TPU v7x, 32 devices: a whole 2x2x4 slice. The times are simulated.
32 devices in a mesh: wave: 8 (over z, core), lev: 4 (over y, x).
Axes of the slice: x: 2, y: 2, z: 4, core: 2. Of those that a mesh axis runs over, the one named last changes fastest.
Arguments:
- spectrum: bfloat16 [4, 4, 2, 1280, 1280], P(None, 'lev', None, 'wave'), may hold values from -6 to 6
- legendre: bfloat16 [1280, 8, 1280], P('wave'), may hold values from -0.15625 to 0.15625
- order_of_slot: int32 [1280], replicated, may hold values from 0 to 1279, each once
- reduced_length: int32 [8], replicated, may hold values from 20 to 5136, as said below
- gauss_weight: float32 [8], P('wave'), may hold values from 2 to 6
- depart_row: int32 [2, 4, 4, 8, 5632], P(None, 'lev', None, 'wave'), may hold values from -1 to 1, as said below
- depart_col: int32 [2, 4, 4, 8, 5632], P(None, 'lev', None, 'wave'), may hold values from 0 to 5135, as said below
- depart_weight: float32 [2, 4, 4, 8, 5632], P(None, 'lev', None, 'wave'), may hold values from 0.05 to 0.5
Outputs:
- spectrum_out: bfloat16 [4, 4, 2, 1280, 1280], P(None, 'lev', None, 'wave')
Inputs may be any that keep to these rules, and one draw needn't show every extreme that they name: `reduced_length`: each latitude j has 20 + 4 i points for a cycle i with j * 160 <= i < (j + 1) * 160; the last latitude has 5136. `depart_row`: offset of the departure latitude from the arrival latitude; a departure latitude outside the window reads zeros. `depart_col`: below the reduced length of the departure latitude (of the nearest window latitude where it lies outside the window). `order_of_slot`: A permutation of the zonal orders.
All inputs are finite; a program needn't handle non-finite values.
Results may differ from a plain program's by a relative error of at most 0.02.
Values may be sent and summed in bfloat16 or wider, within the bound.
A program may use at most 128 MiB of HBM per device.

v0:
```python
import math
import jax
import jax.numpy as jnp
from jax import lax
from jax.sharding import PartitionSpec as P

BLOCK = 512
full_turn = 2.0 * math.pi


def extended_2(block, sides, width):
    for axis, dim in sides:
        count = lax.axis_size(axis)
        forward = [(i, i + 1) for i in range(count - 1)]
        backward = [(target, source) for source, target in forward]
        low = lax.ppermute(
            lax.slice_in_dim(block, block.shape[dim] - width, None, axis=dim), axis, forward
        )
        high = lax.ppermute(lax.slice_in_dim(block, 0, width, axis=dim), axis, backward)
        block = jnp.concatenate([low, block, high], axis=dim)
    return block


def base_table(length, orders, order_limit, block_width):
    offsets = jnp.arange(block_width, dtype=jnp.int32)
    phases = orders[:, None] * offsets[None, :] % length
    angles = phases.astype(jnp.float32) * (jnp.float32(full_turn) / length.astype(jnp.float32))
    active = (orders < order_limit)[:, None]
    cosine = jnp.where(active, jnp.cos(angles), 0.0)
    sine_part = jnp.where(active, -jnp.sin(angles), 0.0)
    return jnp.concatenate([cosine, sine_part], axis=0).astype(jnp.bfloat16)


def block_phases(length, orders, grid_width, block_width):
    starts = jnp.arange(grid_width // block_width, dtype=jnp.int32) * block_width
    phases = starts[:, None] * orders[None, :] % length
    angles = phases.astype(jnp.float32) * (jnp.float32(full_turn) / length.astype(jnp.float32))
    return (jnp.cos(angles), jnp.sin(angles))


def synthesize(coeffs, length, order_limit, fourier_table, cos_phase, sin_phase):
    field_count = coeffs.shape[0]
    blocks = cos_phase.shape[0]
    block_width = fourier_table.shape[1]
    real_part = coeffs[:, 0, :].astype(jnp.float32)[:, None, :]
    imag_part = coeffs[:, 1, :].astype(jnp.float32)[:, None, :]
    rot_real = real_part * cos_phase[None] - imag_part * sin_phase[None]
    rot_imag = real_part * sin_phase[None] + imag_part * cos_phase[None]
    rotated = jnp.stack([rot_real, rot_imag], axis=2).astype(jnp.bfloat16)
    rotated = rotated.reshape(field_count * blocks, -1)
    result = jnp.dot(rotated, fourier_table, preferred_element_type=jnp.float32)
    result = result.reshape(field_count, blocks * block_width)
    points = jnp.arange(blocks * block_width, dtype=jnp.int32)
    factor = 1.0 / jnp.sqrt(order_limit.astype(jnp.float32))
    return jnp.where(points[None, :] < length, result * factor, 0.0)


def analyse(newgrid, fourier_table, cos_phase, sin_phase):
    field_count = newgrid.shape[0]
    blocks = cos_phase.shape[0]
    block_width = fourier_table.shape[1]
    partial_value = lax.dot_general(
        newgrid.reshape(field_count * blocks, block_width),
        fourier_table,
        (((1,), (1,)), ((), ())),
        preferred_element_type=jnp.float32,
    )
    partial_value = partial_value.reshape(field_count, blocks, 2, -1)
    part_real = partial_value[:, :, 0, :]
    part_imag = partial_value[:, :, 1, :]
    real_sum = jnp.sum(part_real * cos_phase[None] + part_imag * sin_phase[None], axis=1)
    imag_sum = jnp.sum(part_imag * cos_phase[None] - part_real * sin_phase[None], axis=1)
    return jnp.stack([real_sum, imag_sum], axis=1)


def per_device(
    spectrum,
    legendre,
    order_of_slot,
    reduced_length,
    gauss_weight,
    depart_row,
    depart_col,
    depart_weight,
):
    own_index = lax.axis_index("wave")
    slot_count = legendre.shape[0]
    orders_total = order_of_slot.shape[0]
    variables = spectrum.shape[0]
    level_count = spectrum.shape[1]
    field_count = variables * level_count
    grid_width = depart_row.shape[-1]
    stencil = depart_row.shape[2]
    own_orders = lax.dynamic_slice_in_dim(order_of_slot, own_index * slot_count, slot_count)
    degrees = jnp.arange(legendre.shape[2], dtype=jnp.int32)
    masked = jnp.where(
        degrees[None, None, :] >= own_orders[:, None, None], legendre, jnp.zeros((), jnp.bfloat16)
    )
    length = lax.dynamic_index_in_dim(reduced_length, own_index, keepdims=False)
    order_limit = jnp.minimum(orders_total, (length - 1) // 2)
    fourier_table = base_table(length, order_of_slot, order_limit, BLOCK)
    cos_phase, sin_phase = block_phases(length, order_of_slot, grid_width, BLOCK)
    own_info = (length, order_limit, fourier_table, cos_phase, sin_phase)
    weight = gauss_weight[0]
    points = jnp.arange(grid_width, dtype=jnp.int32)
    level_base = (jnp.arange(level_count, dtype=jnp.int32) * (3 * grid_width))[:, None, None]
    spectral_state = spectrum
    for step_index in range(depart_row.shape[0]):
        fourier = jnp.einsum(
            "vlcsn,sjn->jvlcs", spectral_state, masked, preferred_element_type=jnp.float32
        ).astype(jnp.bfloat16)
        gathered = lax.all_to_all(fourier, "wave", split_axis=0, concat_axis=4, tiled=True)
        own_grid = synthesize(
            gathered.reshape(field_count, 2, orders_total),
            own_info[0],
            own_info[1],
            own_info[2],
            own_info[3],
            own_info[4],
        )
        extended = extended_2(
            own_grid.reshape(variables, level_count, 1, grid_width).astype(jnp.bfloat16),
            (("wave", 2),),
            1,
        ).astype(jnp.float32)
        flat_rows = extended.reshape(variables, level_count * 3 * grid_width)
        row_offsets = depart_row[step_index][:, :, 0, :]
        columns = depart_col[step_index][:, :, 0, :]
        weights = depart_weight[step_index][:, :, 0, :]
        flat_index = (level_base + (row_offsets + 1) * grid_width + columns).reshape(-1)
        values = jnp.take(flat_rows, flat_index, axis=1)
        values = values.reshape(variables, level_count, stencil, grid_width)
        interp = jnp.sum(values * weights[None], axis=2)
        tendency = interp + 0.5 * jnp.roll(interp, -1, axis=0) * jnp.tanh(
            jnp.roll(interp, -2, axis=0)
        )
        newgrid = jnp.where(points < own_info[0], tendency, 0.0).astype(jnp.bfloat16)
        analysed = analyse(
            newgrid.reshape(field_count, grid_width), own_info[2], own_info[3], own_info[4]
        )
        coeffs = (analysed * (weight * jnp.sqrt(2.0 / own_info[0].astype(jnp.float32)))).astype(
            jnp.bfloat16
        )
        coeffs = coeffs.reshape(1, variables, level_count, 2, orders_total)
        returned = lax.all_to_all(coeffs, "wave", split_axis=4, concat_axis=0, tiled=True)
        spectral_state = jnp.einsum(
            "jvlcs,sjn->vlcsn", returned, masked, preferred_element_type=jnp.float32
        ).astype(jnp.bfloat16)
    return spectral_state


def solution(mesh):
    placed = (
        P(None, "lev", None, "wave", None),
        P("wave", None, None),
        P(),
        P(),
        P("wave"),
        P(None, "lev", None, "wave", None),
        P(None, "lev", None, "wave", None),
        P(None, "lev", None, "wave", None),
    )
    return jax.shard_map(
        per_device,
        mesh=mesh,
        in_specs=placed,
        out_specs=P(None, "lev", None, "wave", None),
        check_vma=False,
    )
```

profile of v0, /device:TPU:0, one launch (start us, length us, event | category | flops | bytes accessed | tf_op | source)
XLA Modules:
  0.0 356.6 jit_solution(9272613454068507887)
XLA Ops:
  0.0 0.9 dynamic_slice.7
  0.9 0.2 iota_compare_fusion
  1.1 0.8 copy-done
  1.9 0.7 copy-done.9
  2.6 5.7 %fusion.31 = bf16[8,4,1,2,160]{0,1,3,4,2:T(4,128)(2,1)} fusion(bf16[4,2,160,1280]{3,2,1,0:T(8,128)(2,1)S(1)} %bitcast.183, bf16[160,8,1280]{2,1,0:T(8,128)(2,1)} %param.11, pred[160,1280]{1,0:T(8,128)(4,1)S(1)} %iota_compare_fusion), kind=kOutput, calls=%fused_computation.38 | convolution fusion | flops 27863040 | bytes 6778880 | tf_op jit(solution)/shard_map/vlcsn,sjn->jvlcs/dot_general | solution.py:109
  8.3 2.0 copy.155
  10.3 6.4 %all-to-all-start = ((bf16[8,4,1,2,160]{4,1,3,2,0:T(4,128)(2,1)}), bf16[8,4,1,2,160]{4,1,3,2,0:T(4,128)(2,1)S(1)}, u32[]{:S(2)}, u32[]{:S(2)}) async-start(bf16[8,4,1,2,160]{4,1,3,2,0:T(4,128)(2,1)} %copy.155), calls=%async_computation | async-start | bytes 65536 | tf_op jit(solution)/shard_map/all_to_all | solution.py:112
  16.6 0.7 dynamic_slice.8
  19.2 1.3 slice_add_fusion
  21.2 1.2 fusion.57
  22.4 36.4 %select_convert_fusion.1 = (bf16[1280,512]{1,0:T(8,128)(2,1)S(1)}, bf16[1280,512]{1,0:T(8,128)(2,1)S(1)}) fusion(f32[]{:T(128)S(6)} %div.18, s32[]{:T(128)S(6)} %select_n.124, s32[1280]{0:T(1024)S(1)} %copy-done.13, pred[1280]{0:T(1024)(128)(4,1)S(1)} %broadcast_compare_fusion, pred[]{:T(512)S(6)} %lt.62), kind=kLoop, calls=%fused_computation.27 | loop fusion | flops 9830400 | bytes 2627849 | tf_op jit(solution)/shard_map/convert.8
  58.9 0.8 copy_bitcast_fusion
  59.7 0.6 iota_compare_fusion.1
  60.6 0.5 subtract_convert_fusion.1
  61.1 0.5 pad_maximum_fusion.1
  61.6 0.2 pad.26
  61.9 0.6 convolution_multiply_fusion.1
  62.5 2.4 collective-permute-start
  64.9 1.5 collective-permute-start.1
  66.4 1.7 pad_maximum_fusion
  68.8 0.3 collective-permute-done.1
  69.3 4.9 %copy.157 = f32[4,1,3,5632]{0,3,2,1:T(8,128)} copy(f32[4,1,3,5632]{3,0,2,1:T(4,128)S(1)} %maximum_convert_fusion) | data formatting | bytes 540672 | tf_op jit(solution)/shard_map/convert_element_type | solution.py:125
  74.2 78.1 %gather_fusion = f32[22528,4]{1,0:T(8,128)} fusion(f32[4,16896]{0,1:T(8,128)} %bitcast.186, s32[22528]{0:T(1024)S(1)} %fusion.60), kind=kCustom, calls=%fused_computation.clone | custom fusion | bytes 811008 | tf_op jit(solution)/shard_map/jit(_take)/gather | solution.py:131
  152.3 12.9 %broadcast_select_fusion.1 = f32[22528,4]{1,0:T(8,128)S(1)} fusion(f32[22528,4]{1,0:T(8,128)} %gather_fusion, pred[22528]{0:T(1024)(128)(4,1)S(1)} %compare_and_fusion.1), kind=kLoop, calls=%fused_computation.5 | loop fusion | flops 90112 | bytes 743424 | tf_op jit(solution)/shard_map/jit(_take)/select_n | solution.py:131
  165.2 3.9 %multiply_reduce_fusion.1 = f32[4,5632]{0,1:T(8,128)S(1)} fusion(f32[4,1,4,5632]{0,3,2,1:T(8,128)S(1)} %bitcast.185, f32[4,5632]{1,0:T(4,128)S(1)} %copy-done.11), kind=kLoop, calls=%fused_computation.3 | loop fusion | flops 157696 | bytes 540672 | tf_op jit(solution)/shard_map/reduce_sum | solution.py:133
  169.1 2.4 slice_bitcast_fusion.1
  171.5 0.8 copy.158
  172.3 0.8 slice_reduce_fusion.1
  173.1 2.8 copy.159
  176.2 0.9 fusion.62
  177.3 0.6 fusion.64
  177.9 2.1 copy.164
  180.0 2.7 reshape.894
  182.7 12.4 %all_to_all.60 = bf16[8,2,640]{2,1,0:T(2,128)(2,1)} all-to-all(bf16[8,2,640]{2,1,0:T(2,128)(2,1)} %reshape.894), channel_id=1, replica_groups=mesh['wave'=8,'lev'=4] {'wave'}, dimensions={0} | all-to-all | bytes 40960 | tf_op jit(solution)/shard_map/all_to_all | solution.py:145
  195.1 2.9 reshape.895
  198.0 4.0 %copy.166 = bf16[1,4,1,2,8,160]{4,1,3,5,2,0:T(4,128)(2,1)} copy(bf16[1,4,1,2,8,160]{1,3,5,4,2,0:T(2,128)(2,1)} %bitcast.191) | data formatting | bytes 40960 | tf_op jit(solution)/shard_map/all_to_all | solution.py:145
  202.0 6.1 %fusion.36 = bf16[8,4,1,2,160]{0,1,3,4,2:T(4,128)(2,1)} fusion(bf16[160,8,1280]{2,1,0:T(8,128)(2,1)S(1)} %copy-done.8, pred[160,1280]{1,0:T(8,128)(4,1)} %copy-done.9, bf16[1,4,1,2,8,160]{4,1,3,5,2,0:T(4,128)(2,1)} %copy.166), kind=kOutput, calls=%fused_computation.39 | convolution fusion | flops 57354240 | bytes 3522560 | tf_op jit(solution)/shard_map/vlcsn,sjn->jvlcs/dot_general | solution.py:109
  208.1 2.1 copy.167
  210.2 3.5 all-to-all-start.2
  213.8 5.4 %all-to-all-done.2 = bf16[8,4,1,2,160]{4,1,3,2,0:T(4,128)(2,1)S(1)} async-done(((bf16[8,4,1,2,160]{4,1,3,2,0:T(4,128)(2,1)}), bf16[8,4,1,2,160]{4,1,3,2,0:T(4,128)(2,1)S(1)}, u32[]{:S(2)}, u32[]{:S(2)}) %all-to-all-start.2) | async-done | bytes 20512 | tf_op jit(solution)/shard_map/all_to_all | solution.py:112
  219.4 0.5 subtract_convert_fusion
  219.9 0.5 pad_maximum_fusion.2
  220.4 0.2 pad.27
  220.6 0.6 convolution_multiply_fusion
  221.3 1.6 collective-permute-start.2
  222.9 1.3 collective-permute-start.3
  224.3 2.3 collective-permute-done.3
  226.7 4.9 %copy.169 = f32[4,1,3,5632]{0,3,2,1:T(8,128)} copy(f32[4,1,3,5632]{3,0,2,1:T(4,128)S(1)} %maximum_convert_fusion.1) | data formatting | bytes 540672 | tf_op jit(solution)/shard_map/convert_element_type | solution.py:125
  231.6 78.1 %gather_fusion.1 = f32[22528,4]{1,0:T(8,128)} fusion(f32[4,16896]{0,1:T(8,128)} %bitcast.187, s32[22528]{0:T(1024)S(1)} %fusion.61), kind=kCustom, calls=%fused_computation.1.clone | custom fusion | bytes 811008 | tf_op jit(solution)/shard_map/jit(_take)/gather | solution.py:131
  309.7 12.9 %broadcast_select_fusion = f32[22528,4]{1,0:T(8,128)S(1)} fusion(f32[22528,4]{1,0:T(8,128)} %gather_fusion.1, pred[22528]{0:T(1024)(128)(4,1)S(1)} %compare_and_fusion), kind=kLoop, calls=%fused_computation.4 | loop fusion | flops 90112 | bytes 743424 | tf_op jit(solution)/shard_map/jit(_take)/select_n | solution.py:131
  322.6 3.9 %multiply_reduce_fusion = f32[4,5632]{0,1:T(8,128)S(1)} fusion(f32[4,1,4,5632]{0,3,2,1:T(8,128)S(1)} %bitcast.184, f32[4,5632]{1,0:T(4,128)S(1)} %copy-done.10), kind=kLoop, calls=%fused_computation.2 | loop fusion | flops 157696 | bytes 540672 | tf_op jit(solution)/shard_map/reduce_sum | solution.py:133
  326.5 2.4 slice_bitcast_fusion
  328.9 0.8 copy.170
  329.7 0.8 slice_reduce_fusion
  330.6 2.8 copy.171
  333.6 0.9 fusion.71
  334.5 0.2 add_reduce_fusion
  334.7 0.5 copy.177
  335.3 1.0 reshape.896
  336.3 9.6 %all_to_all.61 = bf16[8,2,640]{2,1,0:T(2,128)(2,1)S(1)} all-to-all(bf16[8,2,640]{2,1,0:T(2,128)(2,1)S(1)} %reshape.896), channel_id=1, replica_groups=mesh['wave'=8,'lev'=4] {'wave'}, dimensions={0} | all-to-all | bytes 40960 | tf_op jit(solution)/shard_map/all_to_all | solution.py:145
  345.9 1.3 reshape.897
  347.2 3.0 copy.179
  350.2 4.0 %fusion.1 = bf16[4,1,2,160,1280]{4,0,2,3,1:T(4,128)(2,1)S(1)} fusion(bf16[160,8,1280]{2,1,0:T(8,128)(2,1)} %param.11, pred[160,1280]{1,0:T(8,128)(4,1)} %copy-done.9, bf16[1,4,1,2,8,160]{4,1,3,5,2,0:T(4,128)(2,1)} %copy.179), kind=kOutput, calls=%fused_computation.10 | convolution fusion | flops 29491200 | bytes 6778880 | tf_op jit(solution)/shard_map/jvlcs,sjn->vlcsn/dot_general | solution.py:146
  354.3 2.3 copy.180
  (65 shorter events, 1.5 us)
Async XLA Ops:
  0.0 1.9 copy-start
  1.9 0.7 copy-start.9
  2.6 14.0 %copy-start.14 = (s32[8]{0:T(128)S(1)}, s32[8]{0:T(128)}, u32[]{:S(2)}) copy-start(s32[8]{0:T(128)} %param.13) | copy-start | bytes 100
  2.6 18.5 %copy-start.13 = (s32[1280]{0:T(1024)S(1)}, s32[1280]{0:T(1024)}, u32[]{:S(2)}) copy-start(s32[1280]{0:T(1024)} %param.12) | copy-start | bytes 15364
  8.3 50.6 %copy-start.12 = (f32[2,1,4,1,5632]{4,3,2,1,0:T(1,128)S(1)}, f32[2,1,4,1,5632]{4,3,2,1,0:T(1,128)}, u32[]{:S(2)}) copy-start(f32[2,1,4,1,5632]{4,3,2,1,0:T(1,128)} %param.17) | copy-start | bytes 540676
  10.3 50.2 %all-to-all-start = ((bf16[8,4,1,2,160]{4,1,3,2,0:T(4,128)(2,1)}), bf16[8,4,1,2,160]{4,1,3,2,0:T(4,128)(2,1)S(1)}, u32[]{:S(2)}, u32[]{:S(2)}) async-start(bf16[8,4,1,2,160]{4,1,3,2,0:T(4,128)(2,1)} %copy.155), calls=%async_computation | async-start | bytes 65536 | tf_op jit(solution)/shard_map/all_to_all | solution.py:112
  58.9 7.5 %copy-start.4 = (bf16[1280,512]{1,0:T(8,128)(2,1)}, bf16[1280,512]{1,0:T(8,128)(2,1)S(1)}, u32[]{:S(2)}) copy-start(bf16[1280,512]{1,0:T(8,128)(2,1)S(1)} %get-tuple-element.26) | copy-start | bytes 3932164
  58.9 7.5 %copy-start.6 = (bf16[1280,512]{1,0:T(8,128)(2,1)}, bf16[1280,512]{1,0:T(8,128)(2,1)S(1)}, u32[]{:S(2)}) copy-start(bf16[1280,512]{1,0:T(8,128)(2,1)S(1)} %get-tuple-element.27) | copy-start | bytes 3932164
  62.5 6.3 %collective-permute-start = (bf16[4,1,1,5632]{3,0,2,1:T(4,128)(2,1)S(1)}, bf16[4,1,1,5632]{3,0,2,1:T(4,128)(2,1)S(1)}, u32[]{:S(2)}, u32[]{:S(2)}) collective-permute-start(bf16[4,1,1,5632]{3,0,2,1:T(4,128)(2,1)S(1)} %select_convert_fusion.3), channel_id=1, source_target_pairs={{0,4},{4,8},{8,12},{12,16},{16,20},{20,24},{24,28},{1,5},{5,9},{9,... | collective-permute-start | bytes 135176 | tf_op jit(solution)/shard_map/ppermute | solution.py:16
  64.9 4.3 %collective-permute-start.1 = (bf16[4,1,1,5632]{3,0,2,1:T(4,128)(2,1)S(1)}, bf16[4,1,1,5632]{3,0,2,1:T(4,128)(2,1)S(1)}, u32[]{:S(2)}, u32[]{:S(2)}) collective-permute-start(bf16[4,1,1,5632]{3,0,2,1:T(4,128)(2,1)S(1)} %select_convert_fusion.3), channel_id=1, source_target_pairs={{4,0},{8,4},{12,8},{16,12},{20,16},{24,20},{28,24},{5,1},{9,5},{13... | collective-permute-start | bytes 135176 | tf_op jit(solution)/shard_map/ppermute | solution.py:19
  152.3 12.9 %copy-start.11 = (f32[4,5632]{1,0:T(4,128)S(1)}, f32[4,5632]{1,0:T(4,128)}, u32[]{:S(2)}) copy-start(f32[4,5632]{1,0:T(4,128)} %get-tuple-element.33) | copy-start | bytes 270340
  173.1 3.1 copy-start.2
  177.1 24.9 %copy-start.8 = (bf16[160,8,1280]{2,1,0:T(8,128)(2,1)S(1)}, bf16[160,8,1280]{2,1,0:T(8,128)(2,1)}, u32[]{:S(2)}) copy-start(bf16[160,8,1280]{2,1,0:T(8,128)(2,1)} %param.11) | copy-start | bytes 9830404
  208.1 12.5 %copy-start.5 = (bf16[1280,512]{1,0:T(8,128)(2,1)S(1)}, bf16[1280,512]{1,0:T(8,128)(2,1)}, u32[]{:S(2)}) copy-start(bf16[1280,512]{1,0:T(8,128)(2,1)} %copy-done.4) | copy-start | bytes 3932164
  208.1 12.5 %copy-start.7 = (bf16[1280,512]{1,0:T(8,128)(2,1)S(1)}, bf16[1280,512]{1,0:T(8,128)(2,1)}, u32[]{:S(2)}) copy-start(bf16[1280,512]{1,0:T(8,128)(2,1)} %copy-done.6) | copy-start | bytes 3932164
  210.2 9.0 %all-to-all-start.2 = ((bf16[8,4,1,2,160]{4,1,3,2,0:T(4,128)(2,1)}), bf16[8,4,1,2,160]{4,1,3,2,0:T(4,128)(2,1)S(1)}, u32[]{:S(2)}, u32[]{:S(2)}) async-start(bf16[8,4,1,2,160]{4,1,3,2,0:T(4,128)(2,1)} %copy.167), calls=%async_computation.2 | async-start | bytes 65536 | tf_op jit(solution)/shard_map/all_to_all | solution.py:112
  221.3 3.0 collective-permute-start.2
  222.9 3.7 %collective-permute-start.3 = (bf16[4,1,1,5632]{3,0,2,1:T(4,128)(2,1)S(1)}, bf16[4,1,1,5632]{3,0,2,1:T(4,128)(2,1)S(1)}, u32[]{:S(2)}, u32[]{:S(2)}) collective-permute-start(bf16[4,1,1,5632]{3,0,2,1:T(4,128)(2,1)S(1)} %select_convert_fusion.2), channel_id=1, source_target_pairs={{4,0},{8,4},{12,8},{16,12},{20,16},{24,20},{28,24},{5,1},{9,5},{13... | collective-permute-start | bytes 135176 | tf_op jit(solution)/shard_map/ppermute | solution.py:19
  309.7 12.9 %copy-start.10 = (f32[4,5632]{1,0:T(4,128)S(1)}, f32[4,5632]{1,0:T(4,128)}, u32[]{:S(2)}) copy-start(f32[4,5632]{1,0:T(4,128)} %get-tuple-element.32) | copy-start | bytes 270340
  330.6 3.1 copy-start.3
  350.2 6.4 %copy-start.1 = (bf16[4,1,2,160,1280]{4,3,2,1,0:T(8,128)(2,1)S(1)}, bf16[4,1,2,160,1280]{4,3,2,1,0:T(8,128)(2,1)}, u32[]{:S(2)}) copy-start(bf16[4,1,2,160,1280]{4,3,2,1,0:T(8,128)(2,1)} %param.10) | copy-start | bytes 9830404
where the time goes:
time: 357 us
  local copies, waits for them, and re-layouts  209 us (59%)
  other arithmetic  78.6 us (22%)
  blocking collectives  22 us (6%)
  matrix products  18.7 us (5%)
  starting transfers between devices  16.7 us (5%)
  waiting for transfers between devices  8.07 us (2%)
  between operations  3.92 us (1%)
    gather x2, local copies, waits for them, and re-layouts, per_device(): values = jnp.take(flat_rows, flat_index, axis=1)  156 us
    another operation x3, other arithmetic  37.4 us
    select_n x2, other arithmetic, per_device(): values = jnp.take(flat_rows, flat_index, axis=1)  25.7 us
    all_to_all x2, blocking collectives, per_device(): lax.all_to_all(coeffs, 'wave', split_axis=4, concat_axis=0, tiled=True)  22 us
    dot_general x2, matrix products, per_device(): jnp.einsum('vlcsn,sjn->jvlcs', spectral_state, masked, preferred_element_...  11.8 us
    unnamed x42, local copies, waits for them, and re-layouts  10.8 us
    concatenate x6, local copies, waits for them, and re-layouts, per_device(): jnp.roll(interp, -1, axis=0)  10.4 us
    all_to_all x2, starting transfers between devices, per_device(): lax.all_to_all(fourier, 'wave', split_axis=0, concat_axis=4, tiled=True)  9.9 us
  transfers between devices with their start and end apart: 6, of which 3 were waited for; matrix products, arithmetic and copies ran while one was open for 12% of the time, Pallas kernels for 0%

commit v1 on v0

--- a/solution.py
+++ b/solution.py
@@ -142,7 +142,12 @@
             jnp.bfloat16
         )
         coeffs = coeffs.reshape(1, variables, level_count, 2, orders_total)
-        returned = lax.all_to_all(coeffs, "wave", split_axis=4, concat_axis=0, tiled=True)
+        returned = jnp.concatenate(
+            lax.all_to_all(
+                jnp.stack(jnp.split(coeffs, lax.axis_size("wave"), axis=4)), "wave", 0, 0
+            ),
+            axis=0,
+        )
         spectral_state = jnp.einsum(
             "jvlcs,sjn->vlcsn", returned, masked, preferred_element_type=jnp.float32
         ).astype(jnp.bfloat16)

time: 357 us -> 344 us (0.964)
  local copies, waits for them, and re-layouts: 209 us -> 194 us
    unnamed x42 -> x54, local copies, waits for them, and re-layouts: 10.8 us -> 3.74 us
    all_to_all x2, local copies, waits for them, and re-layouts: 6.97 us -> 1.2 us  [per_device(): lax.all_to_all(jnp.stack(jnp.split(coeffs, lax.axis_size('wave'), axis=4)...]
where the time goes in v1:
time: 344 us; the launch traced here: 343 us
  local copies, waits for them, and re-layouts  194 us (56%)
  other arithmetic  77.9 us (23%)
  blocking collectives  21.8 us (6%)
  matrix products  20.5 us (6%)
  starting transfers between devices  16.7 us (5%)
  waiting for transfers between devices  8.07 us (2%)
  between operations  4.06 us (1%)
    gather x2, local copies, waits for them, and re-layouts, per_device(): values = jnp.take(flat_rows, flat_index, axis=1)  157 us
    another operation x3, other arithmetic  37.4 us
    select_n x2, other arithmetic, per_device(): values = jnp.take(flat_rows, flat_index, axis=1)  25.7 us
    all_to_all x2, blocking collectives, per_device(): lax.all_to_all(jnp.stack(jnp.split(coeffs, lax.axis_size('wave'), axis=4)...  21.8 us
    dot_general x2, matrix products, per_device(): jnp.einsum('vlcsn,sjn->jvlcs', spectral_state, masked, preferred_element_...  13.5 us
    concatenate x6, local copies, waits for them, and re-layouts, per_device(): jnp.roll(interp, -1, axis=0)  10.4 us
    convert_element_type x2, local copies, waits for them, and re-layouts, per_device(): extended = extended_2(own_grid.reshape(variables, level_count, 1, grid_wi...  9.9 us
    all_to_all x2, starting transfers between devices, per_device(): lax.all_to_all(fourier, 'wave', split_axis=0, concat_axis=4, tiled=True)  9.69 us
  transfers between devices with their start and end apart: 6, of which 3 were waited for; matrix products, arithmetic and copies ran while one was open for 12% of the time, Pallas kernels for 0%

profile of v1, /device:TPU:0, one launch (start us, length us, event | category | flops | bytes accessed | tf_op | source)
XLA Modules:
  0.0 343.3 jit_solution(4692406887781137849)
XLA Ops:
  0.0 0.9 dynamic_slice.7
  0.9 0.2 iota_compare_fusion
  1.1 0.8 copy-done
  1.9 0.7 copy-done.8
  2.7 5.7 %fusion.31 = bf16[8,4,1,2,160]{0,1,3,4,2:T(4,128)(2,1)} fusion(bf16[4,2,160,1280]{3,2,1,0:T(8,128)(2,1)S(1)} %bitcast.233, bf16[160,8,1280]{2,1,0:T(8,128)(2,1)} %param.11, pred[160,1280]{1,0:T(8,128)(4,1)S(1)} %iota_compare_fusion), kind=kOutput, calls=%fused_computation.38 | convolution fusion | flops 27863040 | bytes 6778880 | tf_op jit(solution)/shard_map/vlcsn,sjn->jvlcs/dot_general | solution.py:109
  8.3 2.0 copy.631
  10.3 6.4 %all-to-all-start = ((bf16[8,4,1,2,160]{4,1,3,2,0:T(4,128)(2,1)}), bf16[8,4,1,2,160]{4,1,3,2,0:T(4,128)(2,1)S(1)}, u32[]{:S(2)}, u32[]{:S(2)}) async-start(bf16[8,4,1,2,160]{4,1,3,2,0:T(4,128)(2,1)} %copy.631), calls=%async_computation | async-start | bytes 65536 | tf_op jit(solution)/shard_map/all_to_all | solution.py:112
  16.7 0.6 dynamic_slice.8
  19.2 1.2 slice_add_fusion
  21.2 1.2 fusion.57
  22.4 36.4 %select_convert_fusion.1 = (bf16[1280,512]{1,0:T(8,128)(2,1)S(1)}, bf16[1280,512]{1,0:T(8,128)(2,1)S(1)}) fusion(f32[]{:T(128)S(6)} %div.18, s32[]{:T(128)S(6)} %select_n.124, s32[1280]{0:T(1024)S(1)} %copy-done.14, pred[1280]{0:T(1024)(128)(4,1)S(1)} %broadcast_compare_fusion, pred[]{:T(512)S(6)} %lt.62), kind=kLoop, calls=%fused_computation.27 | loop fusion | flops 9830400 | bytes 2627849 | tf_op jit(solution)/shard_map/convert.8
  58.9 0.8 copy_bitcast_fusion
  59.7 0.6 iota_compare_fusion.1
  60.5 0.1 reshape.853
  60.6 0.5 subtract_convert_fusion.1
  61.1 0.5 pad_maximum_fusion.1
  61.6 0.2 pad.26
  61.9 0.6 convolution_multiply_fusion.1
  62.5 2.4 collective-permute-start
  64.9 1.5 collective-permute-start.1
  66.4 1.7 pad_maximum_fusion
  68.8 0.3 collective-permute-done.1
  69.2 0.1 maximum_convert_fusion
  69.3 4.9 %copy.633 = f32[4,1,3,5632]{0,3,2,1:T(8,128)} copy(f32[4,1,3,5632]{3,0,2,1:T(4,128)S(1)} %maximum_convert_fusion) | data formatting | bytes 540672 | tf_op jit(solution)/shard_map/convert_element_type | solution.py:125
  74.2 78.5 %gather_fusion = f32[22528,4]{1,0:T(8,128)} fusion(f32[4,16896]{0,1:T(8,128)} %bitcast.236, s32[22528]{0:T(1024)S(1)} %fusion.60), kind=kCustom, calls=%fused_computation.clone | custom fusion | bytes 811008 | tf_op jit(solution)/shard_map/jit(_take)/gather | solution.py:131
  152.7 12.9 %broadcast_select_fusion.1 = f32[22528,4]{1,0:T(8,128)S(1)} fusion(f32[22528,4]{1,0:T(8,128)} %gather_fusion, pred[22528]{0:T(1024)(128)(4,1)S(1)} %compare_and_fusion.1), kind=kLoop, calls=%fused_computation.5 | loop fusion | flops 90112 | bytes 743424 | tf_op jit(solution)/shard_map/jit(_take)/select_n | solution.py:131
  165.6 3.9 %multiply_reduce_fusion.1 = f32[4,5632]{0,1:T(8,128)S(1)} fusion(f32[4,1,4,5632]{0,3,2,1:T(8,128)S(1)} %bitcast.235, f32[4,5632]{1,0:T(4,128)S(1)} %copy-done.11), kind=kLoop, calls=%fused_computation.3 | loop fusion | flops 157696 | bytes 540672 | tf_op jit(solution)/shard_map/reduce_sum | solution.py:133
  169.5 2.4 slice_bitcast_fusion.1
  171.9 0.8 copy.634
  172.7 0.8 slice_reduce_fusion.1
  173.6 2.8 copy.635
  176.4 0.1 fusion.47
  176.6 0.9 fusion.62
  177.5 0.2 add_reduce_fusion.1
  178.4 12.2 %all_to_all.40 = bf16[8,1,4,1,2,160]{5,2,4,3,1,0:T(4,128)(2,1)S(1)} all-to-all(bf16[8,1,4,1,2,160]{5,2,4,3,1,0:T(4,128)(2,1)S(1)} %copy.640), channel_id=1, replica_groups=mesh['wave'=8,'lev'=4] {'wave'}, dimensions={0} | all-to-all | bytes 40960 | tf_op jit(solution)/shard_map/all_to_all | solution.py:146
  190.5 0.2 copy.641
  190.8 7.9 %fusion.36 = bf16[8,4,1,2,160]{0,1,3,4,2:T(4,128)(2,1)} fusion(bf16[160,8,1280]{2,1,0:T(8,128)(2,1)} %param.11, pred[160,1280]{1,0:T(8,128)(4,1)S(1)} %copy-done.9, bf16[8,1,4,1,2,160]{0,2,4,5,3,1:T(4,128)(2,1)S(1)} %copy.641), kind=kOutput, calls=%fused_computation.39 | convolution fusion | flops 57354240 | bytes 3522560 | tf_op jit(solution)/shard_map/vlcsn,sjn->jvlcs/dot_general | solution.py:109
  198.7 2.1 copy.642
  200.7 3.3 all-to-all-start.2
  204.1 5.6 %all-to-all-done.2 = bf16[8,4,1,2,160]{4,1,3,2,0:T(4,128)(2,1)S(1)} async-done(((bf16[8,4,1,2,160]{4,1,3,2,0:T(4,128)(2,1)}), bf16[8,4,1,2,160]{4,1,3,2,0:T(4,128)(2,1)S(1)}, u32[]{:S(2)}, u32[]{:S(2)}) %all-to-all-start.2) | async-done | bytes 20512 | tf_op jit(solution)/shard_map/all_to_all | solution.py:112
  209.8 0.1 reshape.857
  210.0 0.5 subtract_convert_fusion
  210.4 0.5 pad_maximum_fusion.2
  211.0 0.2 pad.27
  211.2 0.6 convolution_multiply_fusion
  211.8 1.6 collective-permute-start.2
  213.5 1.5 collective-permute-start.3
  215.1 2.1 collective-permute-done.3
  217.2 0.1 maximum_convert_fusion.1
  217.3 4.9 %copy.644 = f32[4,1,3,5632]{0,3,2,1:T(8,128)} copy(f32[4,1,3,5632]{3,0,2,1:T(4,128)S(1)} %maximum_convert_fusion.1) | data formatting | bytes 540672 | tf_op jit(solution)/shard_map/convert_element_type | solution.py:125
  222.2 78.5 %gather_fusion.1 = f32[22528,4]{1,0:T(8,128)} fusion(f32[4,16896]{0,1:T(8,128)} %bitcast.237, s32[22528]{0:T(1024)S(1)} %fusion.61), kind=kCustom, calls=%fused_computation.1.clone | custom fusion | bytes 811008 | tf_op jit(solution)/shard_map/jit(_take)/gather | solution.py:131
  300.7 12.9 %broadcast_select_fusion = f32[22528,4]{1,0:T(8,128)S(1)} fusion(f32[22528,4]{1,0:T(8,128)} %gather_fusion.1, pred[22528]{0:T(1024)(128)(4,1)S(1)} %compare_and_fusion), kind=kLoop, calls=%fused_computation.4 | loop fusion | flops 90112 | bytes 743424 | tf_op jit(solution)/shard_map/jit(_take)/select_n | solution.py:131
  313.6 3.9 %multiply_reduce_fusion = f32[4,5632]{0,1:T(8,128)S(1)} fusion(f32[4,1,4,5632]{0,3,2,1:T(8,128)S(1)} %bitcast.234, f32[4,5632]{1,0:T(4,128)S(1)} %copy-done.10), kind=kLoop, calls=%fused_computation.2 | loop fusion | flops 157696 | bytes 540672 | tf_op jit(solution)/shard_map/reduce_sum | solution.py:133
  317.5 2.4 slice_bitcast_fusion
  319.9 0.8 copy.645
  320.7 0.8 slice_reduce_fusion
  321.5 2.8 copy.646
  324.4 0.1 fusion.51
  324.6 0.9 fusion.71
  325.5 0.2 add_reduce_fusion
  326.3 9.6 %all_to_all.41 = bf16[8,1,4,1,2,160]{5,2,4,3,1,0:T(4,128)(2,1)S(1)} all-to-all(bf16[8,1,4,1,2,160]{5,2,4,3,1,0:T(4,128)(2,1)S(1)} %copy.652), channel_id=1, replica_groups=mesh['wave'=8,'lev'=4] {'wave'}, dimensions={0} | all-to-all | bytes 40960 | tf_op jit(solution)/shard_map/all_to_all | solution.py:146
  336.0 1.0 copy.653
  336.9 4.0 %fusion.1 = bf16[4,1,2,160,1280]{4,0,2,3,1:T(4,128)(2,1)S(1)} fusion(bf16[160,8,1280]{2,1,0:T(8,128)(2,1)} %param.11, pred[160,1280]{1,0:T(8,128)(4,1)} %copy-done.8, bf16[8,1,4,1,2,160]{0,2,4,5,3,1:T(4,128)(2,1)} %copy.653), kind=kOutput, calls=%fused_computation.10 | convolution fusion | flops 29491200 | bytes 6778880 | tf_op jit(solution)/shard_map/jvlcs,sjn->vlcsn/dot_general | solution.py:151
  341.0 2.3 copy.654
  (83 shorter events, 1.9 us)
Async XLA Ops:
  0.0 1.9 copy-start
  1.9 0.7 copy-start.8
  2.6 14.0 %copy-start.15 = (s32[8]{0:T(128)S(1)}, s32[8]{0:T(128)}, u32[]{:S(2)}) copy-start(s32[8]{0:T(128)} %param.13) | copy-start | bytes 100
  2.6 16.6 %copy-start.12 = (s32[2,1,4,1,5632]{4,3,2,1,0:T(1,128)S(1)}, s32[2,1,4,1,5632]{4,3,2,1,0:T(1,128)}, u32[]{:S(2)}) copy-start(s32[2,1,4,1,5632]{4,3,2,1,0:T(1,128)} %param.16) | copy-start | bytes 540676
  2.7 18.5 %copy-start.14 = (s32[1280]{0:T(1024)S(1)}, s32[1280]{0:T(1024)}, u32[]{:S(2)}) copy-start(s32[1280]{0:T(1024)} %param.12) | copy-start | bytes 15364
  8.3 50.5 %copy-start.13 = (f32[2,1,4,1,5632]{4,3,2,1,0:T(1,128)S(1)}, f32[2,1,4,1,5632]{4,3,2,1,0:T(1,128)}, u32[]{:S(2)}) copy-start(f32[2,1,4,1,5632]{4,3,2,1,0:T(1,128)} %param.17) | copy-start | bytes 540676
  10.3 50.1 %all-to-all-start = ((bf16[8,4,1,2,160]{4,1,3,2,0:T(4,128)(2,1)}), bf16[8,4,1,2,160]{4,1,3,2,0:T(4,128)(2,1)S(1)}, u32[]{:S(2)}, u32[]{:S(2)}) async-start(bf16[8,4,1,2,160]{4,1,3,2,0:T(4,128)(2,1)} %copy.631), calls=%async_computation | async-start | bytes 65536 | tf_op jit(solution)/shard_map/all_to_all | solution.py:112
  58.9 7.5 %copy-start.4 = (bf16[1280,512]{1,0:T(8,128)(2,1)}, bf16[1280,512]{1,0:T(8,128)(2,1)S(1)}, u32[]{:S(2)}) copy-start(bf16[1280,512]{1,0:T(8,128)(2,1)S(1)} %get-tuple-element.26) | copy-start | bytes 3932164
  58.9 7.5 %copy-start.6 = (bf16[1280,512]{1,0:T(8,128)(2,1)}, bf16[1280,512]{1,0:T(8,128)(2,1)S(1)}, u32[]{:S(2)}) copy-start(bf16[1280,512]{1,0:T(8,128)(2,1)S(1)} %get-tuple-element.27) | copy-start | bytes 3932164
  62.5 6.3 %collective-permute-start = (bf16[4,1,1,5632]{3,0,2,1:T(4,128)(2,1)S(1)}, bf16[4,1,1,5632]{3,0,2,1:T(4,128)(2,1)S(1)}, u32[]{:S(2)}, u32[]{:S(2)}) collective-permute-start(bf16[4,1,1,5632]{3,0,2,1:T(4,128)(2,1)S(1)} %select_convert_fusion.3), channel_id=1, source_target_pairs={{0,4},{4,8},{8,12},{12,16},{16,20},{20,24},{24,28},{1,5},{5,9},{9,... | collective-permute-start | bytes 135176 | tf_op jit(solution)/shard_map/ppermute | solution.py:16
  64.9 4.3 %collective-permute-start.1 = (bf16[4,1,1,5632]{3,0,2,1:T(4,128)(2,1)S(1)}, bf16[4,1,1,5632]{3,0,2,1:T(4,128)(2,1)S(1)}, u32[]{:S(2)}, u32[]{:S(2)}) collective-permute-start(bf16[4,1,1,5632]{3,0,2,1:T(4,128)(2,1)S(1)} %select_convert_fusion.3), channel_id=1, source_target_pairs={{4,0},{8,4},{12,8},{16,12},{20,16},{24,20},{28,24},{5,1},{9,5},{13... | collective-permute-start | bytes 135176 | tf_op jit(solution)/shard_map/ppermute | solution.py:19
  152.7 12.9 %copy-start.11 = (f32[4,5632]{1,0:T(4,128)S(1)}, f32[4,5632]{1,0:T(4,128)}, u32[]{:S(2)}) copy-start(f32[4,5632]{1,0:T(4,128)} %get-tuple-element.33) | copy-start | bytes 270340
  173.6 3.1 copy-start.2
  176.6 14.2 %copy-start.9 = (pred[160,1280]{1,0:T(8,128)(4,1)S(1)}, pred[160,1280]{1,0:T(8,128)(4,1)}, u32[]{:S(2)}) copy-start(pred[160,1280]{1,0:T(8,128)(4,1)} %copy-done.8) | copy-start | bytes 614404
  198.7 12.5 %copy-start.5 = (bf16[1280,512]{1,0:T(8,128)(2,1)S(1)}, bf16[1280,512]{1,0:T(8,128)(2,1)}, u32[]{:S(2)}) copy-start(bf16[1280,512]{1,0:T(8,128)(2,1)} %copy-done.4) | copy-start | bytes 3932164
  198.7 12.5 %copy-start.7 = (bf16[1280,512]{1,0:T(8,128)(2,1)S(1)}, bf16[1280,512]{1,0:T(8,128)(2,1)}, u32[]{:S(2)}) copy-start(bf16[1280,512]{1,0:T(8,128)(2,1)} %copy-done.6) | copy-start | bytes 3932164
  200.7 9.0 %all-to-all-start.2 = ((bf16[8,4,1,2,160]{4,1,3,2,0:T(4,128)(2,1)}), bf16[8,4,1,2,160]{4,1,3,2,0:T(4,128)(2,1)S(1)}, u32[]{:S(2)}, u32[]{:S(2)}) async-start(bf16[8,4,1,2,160]{4,1,3,2,0:T(4,128)(2,1)} %copy.642), calls=%async_computation.2 | async-start | bytes 65536 | tf_op jit(solution)/shard_map/all_to_all | solution.py:112
  211.8 3.2 collective-permute-start.2
  213.5 3.7 %collective-permute-start.3 = (bf16[4,1,1,5632]{3,0,2,1:T(4,128)(2,1)S(1)}, bf16[4,1,1,5632]{3,0,2,1:T(4,128)(2,1)S(1)}, u32[]{:S(2)}, u32[]{:S(2)}) collective-permute-start(bf16[4,1,1,5632]{3,0,2,1:T(4,128)(2,1)S(1)} %select_convert_fusion.2), channel_id=1, source_target_pairs={{4,0},{8,4},{12,8},{16,12},{20,16},{24,20},{28,24},{5,1},{9,5},{13... | collective-permute-start | bytes 135176 | tf_op jit(solution)/shard_map/ppermute | solution.py:19
  300.7 12.9 %copy-start.10 = (f32[4,5632]{1,0:T(4,128)S(1)}, f32[4,5632]{1,0:T(4,128)}, u32[]{:S(2)}) copy-start(f32[4,5632]{1,0:T(4,128)} %get-tuple-element.32) | copy-start | bytes 270340
  321.5 3.1 copy-start.3
  336.9 6.4 %copy-start.1 = (bf16[4,1,2,160,1280]{4,3,2,1,0:T(8,128)(2,1)S(1)}, bf16[4,1,2,160,1280]{4,3,2,1,0:T(8,128)(2,1)}, u32[]{:S(2)}) copy-start(bf16[4,1,2,160,1280]{4,3,2,1,0:T(8,128)(2,1)} %param.10) | copy-start | bytes 9830404
